TPU v7x, 32 devices: a whole 2x2x4 slice. The times are simulated.
32 devices in a mesh: sample: 16 (over z, x, core), basis: 2 (over y).
Axes of the slice: x: 2, y: 2, z: 4, core: 2. Of those that a mesh axis runs over, the one named last changes fastest.
Arguments:
- points: float32 [10, 32768], P(None, 'sample'), may hold values from -1 to 1
- run_weights: float32 [32768], P('sample'), may hold values from 0.25 to 6.1
- panel_degrees: int32 [10, 128], P(None, 'basis'), may hold values from 0 to 6, as said below
- trailing_degrees: int32 [10, 512], P(None, 'basis'), may hold values from 0 to 6, as said below
Outputs:
- r_factor: float32 [128, 128], replicated
- coupling: float32 [128, 512], P(None, 'basis')
- updated: float32 [32768, 512], P('sample', 'basis')
Inputs may be any that keep to these rules, and one draw needn't show every extreme that they name: `panel_degrees`: every column is a multi-index of total degree at most 6; all 640 columns are distinct. `trailing_degrees`: as for panel_degrees; no trailing column repeats a panel column.
All inputs are finite; a program needn't handle non-finite values.
Results may differ from a plain program's by a relative error of at most 0.0003.
Values sent between devices are 32-bit elements; how exact they have to be, the bound alone decides.
No kernel may reach another device: no remote copies, remote signals or barrier semaphores. Data moves between devices by JAX's collectives and lax.ppermute only.
A program may use at most 64 MiB of HBM per device.

v0:
```python
import math

import jax
import jax.numpy as jnp
from jax import lax
from jax.sharding import PartitionSpec as P

DEG = 6


def legendre_rows(coord):
    values = [jnp.ones_like(coord), coord]
    for degree in range(1, DEG):
        values.append(
            ((2.0 * degree + 1.0) * coord * values[degree] - degree * values[degree - 1])
            / (degree + 1.0)
        )
    return jnp.stack(
        [values[degree] * math.sqrt(2.0 * degree + 1.0) for degree in range(DEG + 1)], axis=0
    )


def weighted_columns(points, degrees, weights, run_total):
    levels = jnp.arange(DEG + 1, dtype=jnp.int32)
    product = jnp.broadcast_to(
        jnp.sqrt(weights / run_total)[:, None], (weights.shape[0], degrees.shape[1])
    )
    for dim_index in range(points.shape[0]):
        table = legendre_rows(points[dim_index])
        selector = (degrees[dim_index][None, :] == levels[:, None]).astype(jnp.float32)
        product = product * lax.dot_general(
            table, selector, (((0,), (0,)), ((), ())), precision=lax.Precision.HIGHEST
        )
    return product


def inner_products(left, right):
    return lax.dot_general(left, right, (((0,), (0,)), ((), ())), precision=lax.Precision.HIGHEST)


def shards(points, run_weights, panel_degrees, trailing_degrees):
    run_count = points.shape[1] * lax.axis_size("sample")
    run_total = float(run_count)
    own_columns = weighted_columns(points, panel_degrees, run_weights, run_total)
    panel = lax.all_gather(own_columns, "basis", axis=1, tiled=True)
    trailing = weighted_columns(points, trailing_degrees, run_weights, run_total)
    width = panel.shape[1]
    identity = jnp.eye(width, dtype=jnp.float32)
    gram_matrix, cross_terms = lax.psum(
        (inner_products(panel, panel), inner_products(panel, trailing)), "sample"
    )
    lower_factor = jnp.linalg.cholesky(gram_matrix)
    inverse_lower = jax.scipy.linalg.solve_triangular(lower_factor, identity, lower=True)
    ortho_rows = lax.dot_general(
        inverse_lower, panel, (((1,), (1,)), ((), ())), precision=lax.Precision.HIGHEST
    )
    coupling = jnp.dot(inverse_lower, cross_terms, precision=lax.Precision.HIGHEST)
    updated = (trailing - inner_products(ortho_rows, coupling)) * math.sqrt(run_count)
    return (lower_factor.T, coupling, updated)


def solution(mesh):
    in_specs = (P(None, "sample"), P("sample"), P(None, "basis"), P(None, "basis"))
    out_specs = (P(), P(None, "basis"), P("sample", "basis"))
    return jax.shard_map(shards, mesh=mesh, in_specs=in_specs, out_specs=out_specs, check_vma=False)
```

profile of v0, /device:TPU:0, one launch (start us, length us, event | category | flops | bytes accessed | tf_op | source)
XLA Modules:
  0.0 177.4 jit_solution(13644355350726908377)
XLA Ops:
  7.2 1.5 broadcast_multiply_fusion.40
  8.7 2.1 %subtract_multiply_fusion = (f32[1,2048]{1,0:T(1,128)S(1)}, f32[1,2048]{1,0:T(1,128)S(1)}, f32[1,2048]{1,0:T(1,128)S(1)}, f32[1,2048]{1,0:T(1,128)S(1)}, f32[1,2...) fusion(f32[10,2048]{1,0:T(8,128)} %param.4), kind=kLoop, calls=%fused_computation.62 | loop fusion | flops 509952 | bytes 483328 | tf_op jit(solution)/shard_map/mul | solution.py:19
  10.8 1.0 slice_bitcast_fusion
  11.8 0.7 multiply_sqrt_fusion
  14.1 0.4 convolution_multiply_fusion.17
  15.6 0.4 convolution_multiply_fusion.14
  16.1 0.4 convolution_multiply_fusion.13
  17.7 1.2 convolution_multiply_fusion.10
  19.2 1.2 convolution_multiply_fusion.9
  20.4 1.0 convolution_multiply_fusion.8
  21.5 1.0 convolution_multiply_fusion.7
  22.5 1.1 convolution_multiply_fusion.6
  23.6 1.0 convolution_multiply_fusion.5
  24.6 1.0 convolution_multiply_fusion.4
  25.7 1.1 convolution_multiply_fusion.3
  26.7 1.0 convolution_multiply_fusion.2
  27.8 1.0 convolution_multiply_fusion.1
  28.8 1.0 convolution_multiply_fusion
  29.9 13.2 %all-gather.2.cloned.1.call-done = f32[2048,128]{0,1:T(8,128)} async-done(((f32[2048,64]{0,1:T(8,128)}), f32[2048,128]{0,1:T(8,128)}) %all-gather.2.cloned.1.call-update) | async-done | bytes 1048592 | tf_op jit(solution)/shard_map/all_gather | solution.py:45
  43.1 3.3 %fusion.36 = f32[128,128]{0,1:T(8,128)} fusion(f32[2048,128]{0,1:T(8,128)} %all-gather.2.cloned.1.call-done), kind=kOutput, calls=%fused_computation.195 | convolution fusion | flops 402653184 | bytes 1114112 | tf_op jit(solution)/shard_map/dot_general | solution.py:38
  46.4 2.0 %fusion.37 = f32[128,256]{1,0:T(8,128)} fusion(f32[2048,128]{0,1:T(8,128)S(1)} %copy-done, f32[2048,256]{1,0:T(8,128)S(1)} %convolution_multiply_fusion), kind=kOutput, calls=%fused_computation.196 | convolution fusion | flops 805306368 | bytes 3276800 | tf_op jit(solution)/shard_map/dot_general | solution.py:38
  48.4 91.0 %all-reduce.3.cloned.1.call-done = (f32[128,128]{0,1:T(8,128)}, f32[128,256]{1,0:T(8,128)}) async-done(((f32[128,128]{0,1:T(8,128)}, f32[128,256]{1,0:T(8,128)}), (f32[128,128]{0,1:T(8,128)}, f32[128,256]{1,0:T(8,128)})) %all-reduce.3.cloned.1.call-update) | async-done | bytes 196624 | tf_op jit(solution)/shard_map/psum | solution.py:49
  139.5 0.9 copy.8
  140.4 0.9 fusion.3
  141.3 11.7 %cholesky.20 = f32[128,128]{1,0:T(8,128)S(1)} custom-call(f32[128,128]{1,0:T(8,128)S(1)} %fusion.3), custom_call_target="Cholesky" | custom-call | tf_op jit(solution)/shard_map/jit(cholesky)/cholesky | solution.py:52
  153.0 0.6 compare_reduce_fusion
  153.7 0.7 select_bitcast_fusion
  154.3 9.8 %custom-call.7 = f32[1,128,128]{1,2,0:T(8,128)S(1)} custom-call(f32[1,128,128]{2,1,0:T(8,128)S(1)} %get-tuple-element.104), custom_call_target="InvertDiagBlocksLowerTriangular" | custom-call | tf_op jit(solution)/shard_map/jit(_solve_triangular)/triangular_solve | solution.py:53
  164.4 0.7 copy.9
  165.1 1.2 fusion.38
  166.3 1.0 fusion.39
  167.3 3.2 %fusion = f32[2048,256]{1,0:T(8,128)} fusion(f32[2048,256]{1,0:T(8,128)S(1)} %convolution_multiply_fusion, f32[128,2048]{1,0:T(8,128)S(1)} %fusion.39, f32[128,256]{1,0:T(8,128)S(1)} %fusion.38), kind=kOutput, calls=%fused_computation.11 | convolution fusion | flops 806354944 | bytes 5373952 | tf_op jit(solution)/shard_map/dot_general | solution.py:38
  (45 shorter events, 4.4 us)
Async XLA Ops:
  7.2 36.0 %all-gather.2.cloned.1.call-start = ((), (), s32[]{:S(2)}) async-start(), calls=%async_computation | async-start | bytes 1572864 | tf_op jit(solution)/shard_map/all_gather | solution.py:45
  16.7 2.5 %copy-start.2 = (s32[10,256]{1,0:T(8,128)S(1)}, s32[10,256]{1,0:T(8,128)}, u32[]{:S(2)}) copy-start(s32[10,256]{1,0:T(8,128)} %param.7) | copy-start | bytes 30724
  19.0 120.5 %all-reduce.3.cloned.1.call-start = ((), (), s32[]{:S(2)}) async-start(), calls=%async_computation.1 | async-start | bytes 393216 | tf_op jit(solution)/shard_map/psum | solution.py:49
  43.1 3.3 %copy-start = (f32[2048,128]{0,1:T(8,128)S(1)}, f32[2048,128]{0,1:T(8,128)}, u32[]{:S(2)}) copy-start(f32[2048,128]{0,1:T(8,128)} %all-gather.2.cloned.1.call-done) | copy-start | bytes 3145732
  166.3 4.2 %copy-start.1 = (f32[128,256]{1,0:T(8,128)}, f32[128,256]{1,0:T(8,128)S(1)}, u32[]{:S(2)}) copy-start(f32[128,256]{1,0:T(8,128)S(1)} %fusion.38) | copy-start | bytes 393220
Sparse Core Ops, SparseCore 0:
  19.1 24.0 all-gather.1
  48.6 90.8 all-reduce.2
where the time goes:
time: 178 us; the launch traced here: 177 us
  waiting for transfers between devices  104 us (58%)
  other arithmetic  28.3 us (16%)
  matrix products  26.5 us (15%)
  between operations  14.4 us (8%)
  local copies, waits for them, and re-layouts  3.65 us (2%)
    psum x1, waiting for transfers between devices, shards(): lax.psum((inner_products(panel, panel), inner_products(panel, trailing)),...  91 us
    dot_general x20, matrix products, weighted_columns(): lax.dot_general(table, selector, (((0,), (0,)), ((), ())), precision=lax....  15.6 us
    all_gather x1, waiting for transfers between devices, shards(): panel = lax.all_gather(own_columns, 'basis', axis=1, tiled=True)  13.2 us
    another operation x3, other arithmetic, shards(): lower_factor = jnp.linalg.cholesky(gram_matrix)  12.4 us
    another operation x2, other arithmetic, shards(): jax.scipy.linalg.solve_triangular(lower_factor, identity, lower=True)  10.5 us
    dot_general x3, matrix products, inner_products(): lax.dot_general(left, right, (((0,), (0,)), ((), ())), precision=lax.Prec...  8.48 us
    mul x17, other arithmetic, legendre_rows(): values[degree] * math.sqrt(2.0 * degree + 1.0)  3.87 us
  transfers between devices with their start and end apart: 2, of which 2 were waited for; matrix products, arithmetic and copies ran while one was open for 6% of the time, Pallas kernels for 0%

commit v1 on v0

v1 whole, which is shorter than its diff:
```python
import functools
import math

import jax
import jax.numpy as jnp
from jax import lax
from jax.experimental import pallas as pl
from jax.experimental.pallas import tpu as pltpu
from jax.sharding import PartitionSpec as P

DEG = 6
LANES = 128
F32 = jnp.float32
BF16 = jnp.bfloat16
HIGHEST = lax.Precision.HIGHEST


def rank3(a, b, c):
    all3, last2 = a + b + c, b + c
    return all3 * (all3 + 1) * (all3 + 2) // 6 + last2 * (last2 + 1) // 2 + c


def rank4(a, b, c, d):
    all4 = a + b + c + d
    return all4 * (all4 + 1) * (all4 + 2) * (all4 + 3) // 24 + rank3(b, c, d)


def codes(degrees, rows):
    d = [degrees[i] for i in range(degrees.shape[0])]
    return rows * jnp.stack([rank3(*d[0:3]), rank3(*d[3:6]), rank4(*d[6:10])])


def split2(x):
    high = x.astype(BF16)
    return high, (x - high.astype(F32)).astype(BF16)


def dot3(left, right, dims):
    (lh, ll), (rh, rl) = left, right
    go = functools.partial(lax.dot_general, dimension_numbers=(dims, ((), ())), preferred_element_type=F32)
    return go(lh, rh) + go(lh, rl) + go(ll, rh)


def levels(p):
    one = jnp.ones_like(p)
    v = [one, p]
    for k in range(1, DEG):
        v.append(((2.0 * k + 1.0) * p * v[k] - float(k) * v[k - 1]) * (1.0 / (k + 1.0)))
    return [one] + [v[k] * math.sqrt(2.0 * k + 1.0) for k in range(1, DEG + 1)]


def times(x, factor, degree):
    return x * factor[degree] if degree else x


def basis_gram(run_total, cp, ct, pts, wts, gram, basis, tab_a, tab_b, tab_c, coord, sel):
    rows = wts.shape[0]
    for d in range(pts.shape[0]):
        for i in range(rows):
            coord[pl.ds(d * rows + i, 1), :] = pts[pl.ds(d, 1), pl.ds(i * LANES, LANES)]
    scale = jnp.sqrt(wts[...] / run_total)
    lv = [levels(coord[pl.ds(d * rows, rows), :]) for d in range(pts.shape[0])]

    def put(table, rank, value):
        table[pl.ds(rank * rows, rows), :] = value

    for table, d, first in ((tab_a, 0, scale), (tab_b, 3, jnp.ones_like(scale))):
        for a in range(DEG + 1):
            xa = times(first, lv[d], a)
            for b in range(DEG + 1 - a):
                xb = times(xa, lv[d + 1], b)
                for c in range(DEG + 1 - a - b):
                    put(table, rank3(a, b, c), times(xb, lv[d + 2], c))
    for a in range(DEG + 1):
        xa = lv[6][a]
        for b in range(DEG + 1 - a):
            xb = times(xa, lv[7], b)
            for c in range(DEG + 1 - a - b):
                xc = times(xb, lv[8], c)
                for d in range(DEG + 1 - a - b - c):
                    put(tab_c, rank4(a, b, c, d), times(xc, lv[9], d))
    width, others = cp.shape[1], ct.shape[1]

    def select(code, base, count):
        unroll = 8

        def body(t, carry):
            for u in range(unroll):
                j = t * unroll + u
                a, b, c = (pl.multiple_of(code[g, j], rows) for g in range(3))
                value = tab_a[pl.ds(a, rows), :] * tab_b[pl.ds(b, rows), :] * tab_c[pl.ds(c, rows), :]
                sel[pl.ds(pl.multiple_of((base + j) * rows, rows), rows), :] = value
            return carry

        lax.fori_loop(0, count // unroll, body, 0)

    select(cp, 0, width)
    select(ct, width, others)
    total = width + others
    acc = jnp.zeros((width, total), F32)
    for i in range(rows // 2):
        x = jnp.concatenate([sel[pl.ds(2 * i + h, total, stride=rows), :] for h in range(2)], axis=1)
        basis[:, pl.ds(2 * i * LANES, 2 * LANES)] = x
        high, low = split2(x)
        acc = acc + dot3((high[:width], low[:width]), (high, low), ((1,), (1,)))
    gram[...] = acc


def factor(scale, total_ref, r_out, coupling_out, mix_out, work):
    n = total_ref.shape[0]
    block = 8
    lane = lax.broadcasted_iota(jnp.int32, (n, n), 1)
    row = lax.broadcasted_iota(jnp.int32, (n, n), 0)
    work[:, :n] = total_ref[:, :n]
    work[:, n:] = (lane == row).astype(F32)
    sub = lax.broadcasted_iota(jnp.int32, (block, n), 0)
    for k in range(n // block):
        lo = k * block
        ar = work[lo : lo + block, :]
        e = {}
        for c in range(block):
            col = jnp.broadcast_to(ar[:, lo + c : lo + c + 1], (block, n))
            for r in range(c, block):
                e[r, c] = jnp.broadcast_to(col[r : r + 1, :], (block, n))
        z, inv = {}, []
        for r in range(block):
            inv.append(lax.rsqrt(e[r, r]))
            recip = inv[r] * inv[r]
            m = {q: e[q, r] * recip for q in range(r + 1, block)}
            for q in range(r + 1, block):
                for c in range(r + 1, q + 1):
                    e[q, c] = e[q, c] - m[q] * e[c, r]
                for c in range(r):
                    z[q, c] = z[q, c] - m[q] * z[r, c]
                z[q, r] = -m[q]
        out = None
        for c in range(block):
            col = jnp.where(sub == c, inv[c], 0.0)
            for r in range(c + 1, block):
                col = jnp.where(sub == r, z[r, c] * inv[r], col)
            term = jnp.concatenate([col, col], axis=1) * jnp.broadcast_to(ar[c : c + 1, :], (block, 2 * n))
            out = term if out is None else out + term
        work[lo : lo + block, :] = out
        if k < n // block - 1:
            after = lo + block
            work[after:, :] = work[after:, :] - lax.dot_general(
                out[:, after:n], out, (((0,), (0,)), ((), ())), preferred_element_type=F32, precision=HIGHEST
            )
    r_out[...] = jnp.where(lane >= row, work[:, :n], 0.0)
    inverse = work[:, n:]
    coupling = jnp.dot(inverse, total_ref[:, n:], preferred_element_type=F32, precision=HIGHEST)
    coupling_out[...] = coupling
    mix_out[...] = scale * lax.dot_general(
        inverse, coupling, (((0,), (0,)), ((), ())), preferred_element_type=F32, precision=HIGHEST
    )


def update(scale, basis, mix, out):
    width = mix.shape[0]
    x = basis[...]
    out[...] = x[width:].T * scale - dot3(split2(x[:width]), split2(mix[...]), ((0,), (0,)))


def butterfly(x, axis, steps):
    size = lax.axis_size(axis)
    for step in steps:
        x = x + lax.ppermute(x, axis, [(i, i ^ step) for i in range(size)])
    return x


def powers(size):
    return [1 << b for b in range(size.bit_length() - 1)]


def all_sum(x, axis):
    size = lax.axis_size(axis)
    if size & (size - 1):
        return lax.psum(x, axis)
    if size == 1:
        return x
    half = x.shape[0] // 2
    odd = lax.axis_index(axis) % 2
    swap = [(i, i ^ 1) for i in range(size)]
    mine = lax.dynamic_slice_in_dim(x, odd * half, half, 0)
    mine = mine + lax.ppermute(lax.dynamic_slice_in_dim(x, (1 - odd) * half, half, 0), axis, swap)
    mine = butterfly(mine, axis, powers(size)[1:])
    other = lax.ppermute(mine, axis, swap)
    return jnp.where(odd == 0, jnp.concatenate([mine, other]), jnp.concatenate([other, mine]))


def gather_columns(x, axis):
    size = lax.axis_size(axis)
    if size & (size - 1):
        return lax.all_gather(x, axis, axis=1, tiled=True)
    full = jnp.zeros((x.shape[0], x.shape[1] * size), x.dtype)
    full = lax.dynamic_update_slice_in_dim(full, x, lax.axis_index(axis) * x.shape[1], 1)
    return butterfly(full, axis, powers(size))


def shards(points, run_weights, panel_degrees, trailing_degrees):
    runs = points.shape[1]
    rows = runs // LANES
    run_total = runs * lax.axis_size("sample")
    scale = math.sqrt(run_total)
    panel_codes = gather_columns(codes(panel_degrees, rows), "basis")
    trailing_codes = codes(trailing_degrees, rows)
    width, others = panel_codes.shape[1], trailing_codes.shape[1]
    total = width + others
    smem = pl.BlockSpec(memory_space=pltpu.SMEM)
    vmem = pl.BlockSpec(memory_space=pltpu.VMEM)
    gram, basis = pl.pallas_call(
        functools.partial(basis_gram, float(run_total)),
        out_shape=[jax.ShapeDtypeStruct((width, total), F32), jax.ShapeDtypeStruct((total, runs), F32)],
        in_specs=[smem, smem, vmem, vmem],
        out_specs=[vmem, vmem],
        scratch_shapes=[
            pltpu.VMEM((84 * rows, LANES), F32),
            pltpu.VMEM((84 * rows, LANES), F32),
            pltpu.VMEM((210 * rows, LANES), F32),
            pltpu.VMEM((points.shape[0] * rows, LANES), F32),
            pltpu.VMEM((total * rows, LANES), F32),
        ],
        compiler_params=pltpu.CompilerParams(vmem_limit_bytes=20 << 20),
        name="basis_gram",
    )(panel_codes, trailing_codes, points, run_weights.reshape(rows, LANES))
    sums = all_sum(gram, "sample")
    r_factor, coupling, mix = pl.pallas_call(
        functools.partial(factor, scale),
        out_shape=[
            jax.ShapeDtypeStruct((width, width), F32),
            jax.ShapeDtypeStruct((width, others), F32),
            jax.ShapeDtypeStruct((width, others), F32),
        ],
        in_specs=[vmem],
        out_specs=[vmem, vmem, vmem],
        scratch_shapes=[pltpu.VMEM((width, 2 * width), F32)],
        compiler_params=pltpu.CompilerParams(vmem_limit_bytes=20 << 20),
        name="factor",
    )(sums)
    tile = 2 * LANES
    updated = pl.pallas_call(
        functools.partial(update, scale),
        out_shape=jax.ShapeDtypeStruct((runs, others), F32),
        grid=(runs // tile,),
        in_specs=[pl.BlockSpec((total, tile), lambda i: (0, i)), pl.BlockSpec((width, others), lambda i: (0, 0))],
        out_specs=pl.BlockSpec((tile, others), lambda i: (i, 0)),
        compiler_params=pltpu.CompilerParams(vmem_limit_bytes=20 << 20),
        name="update",
    )(basis, mix)
    return (r_factor, coupling, updated)


def solution(mesh):
    in_specs = (P(None, "sample"), P("sample"), P(None, "basis"), P(None, "basis"))
    out_specs = (P(), P(None, "basis"), P("sample", "basis"))
    return jax.shard_map(shards, mesh=mesh, in_specs=in_specs, out_specs=out_specs, check_vma=False)
```

time: 178 us -> 45.5 us (0.26)
  waiting for transfers between devices: 104 us -> 11.6 us
  matrix products: 26.5 us -> 0 us
  other arithmetic: 28.3 us -> 2.22 us
  Pallas kernels: 0 us -> 18.5 us
  between operations: 14.4 us -> 0.77 us
  starting transfers between devices: 0.26 us -> 10.1 us
  local copies, waits for them, and re-layouts: 3.65 us -> 1.85 us
    psum x1 -> x0, waiting for transfers between devices: 91 us -> none  [shards(): lax.psum((inner_products(panel, panel), inner_products(panel, trailing)),...]
    dot_general x25 -> x0, matrix products: 26.2 us -> none  [the longest x20 15.6 us: weighted_columns(): lax.dot_general(table, selector, (((0,), (0,)), ((), ())), precision=lax....]
    another operation x5 -> x0, other arithmetic: 22.9 us -> none  [the longest x3 12.4 us: shards(): lower_factor = jnp.linalg.cholesky(gram_matrix)]
    pallas_call x0 -> x3, Pallas kernels: none -> 18.5 us  [the longest x1 9.52 us: shards(): pl.pallas_call(functools.partial(factor, scale), out_shape=[jax.ShapeDtyp...]
    all_gather x1 -> x0, waiting for transfers between devices: 13.2 us -> none  [shards(): panel = lax.all_gather(own_columns, 'basis', axis=1, tiled=True)]
    ppermute x0 -> x6, waiting for transfers between devices: none -> 11.6 us  [the longest x4 9.06 us: butterfly(): x = x + lax.ppermute(x, axis, [(i, i ^ step) for i in range(size)])]
    ppermute x0 -> x6, starting transfers between devices: none -> 10.1 us  [the longest x4 9.91 us: butterfly(): x = x + lax.ppermute(x, axis, [(i, i ^ step) for i in range(size)])]
    mul x17 -> x2, other arithmetic: 3.87 us -> 0.02 us  [codes(): return rows * jnp.stack([rank3(*d[0:3]), rank3(*d[3:6]), rank4(*d[6:10])])]
  transfers between devices with their start and end apart: 2 -> 6, of which waited for: 2 -> 6; matrix products, arithmetic and copies ran while one was open for 6% -> 2% of each run, Pallas kernels for 0% -> 0%
where the time goes in v1:
time: 45.5 us; the launch traced here: 45 us
  Pallas kernels  18.5 us (41%)
  waiting for transfers between devices  11.6 us (25%)
  starting transfers between devices  10.1 us (22%)
  other arithmetic  2.22 us (5%)
  local copies, waits for them, and re-layouts  1.85 us (4%)
  between operations  0.77 us (2%)
    ppermute x4, starting transfers between devices, butterfly(): x = x + lax.ppermute(x, axis, [(i, i ^ step) for i in range(size)])  9.91 us
    pallas_call x1, Pallas kernels, shards(): pl.pallas_call(functools.partial(factor, scale), out_shape=[jax.ShapeDtyp...  9.52 us
    ppermute x4, waiting for transfers between devices, butterfly(): x = x + lax.ppermute(x, axis, [(i, i ^ step) for i in range(size)])  9.06 us
    pallas_call x1, Pallas kernels, shards(): pl.pallas_call(functools.partial(basis_gram, float(run_total)), out_shape...  4.54 us
    pallas_call x1, Pallas kernels, shards(): pl.pallas_call(functools.partial(update, scale), out_shape=jax.ShapeDtype...  4.45 us
    add x2, other arithmetic, rank3(): return all3 * (all3 + 1) * (all3 + 2) // 6 + last2 * (last2 + 1) // 2 + c  2.06 us
    unnamed x4, local copies, waits for them, and re-layouts  1.6 us
    ppermute x1, waiting for transfers between devices, all_sum(): other = lax.ppermute(mine, axis, swap)  1.28 us
  transfers between devices with their start and end apart: 6, of which 6 were waited for; matrix products, arithmetic and copies ran while one was open for 2% of the time, Pallas kernels for 0%

profile of v1, /device:TPU:0, one launch (start us, length us, event | category | flops | bytes accessed | tf_op | source)
XLA Modules:
  0.0 45.0 jit_solution(14799311360684173487)
XLA Ops:
  0.6 1.0 %add_add_fusion.5 = (s32[1,64]{1,0:T(1,128)S(1)}, s32[1,64]{1,0:T(1,128)S(1)}, s32[1,64]{1,0:T(1,128)S(1)}) fusion(s32[10,64]{1,0:T(8,128)} %param.6), kind=kLoop, calls=%fused_computation.67 | loop fusion | flops 7680 | bytes 3328 | tf_op jit(solution)/shard_map/add | solution.py:20
  1.7 0.1 dynamic_update_slice.5
  1.8 3.1 %collective-permute-start = (s32[3,128]{1,0:T(4,128)S(1)}, s32[3,128]{1,0:T(4,128)S(1)}, u32[]{:S(2)}, u32[]{:S(2)}) collective-permute-start(s32[3,128]{1,0:T(4,128)S(1)} %dynamic_update_slice.5), channel_id=1, source_target_pairs={{0,1},{1,0},{2,3},{3,2},{4,5},{5,4},{6,7},{7,6},{8,9},{9,8},{10,11... | collective-permute-start | bytes 4616 | tf_op jit(solution)/shard_map/ppermute | solution.py:167
  5.0 1.0 %add_add_fusion.2 = (s32[1,256]{1,0:T(1,128)S(1)}, s32[1,256]{1,0:T(1,128)S(1)}, s32[1,256]{1,0:T(1,128)S(1)}) fusion(s32[10,256]{1,0:T(8,128)} %param.7), kind=kLoop, calls=%fused_computation.51 | loop fusion | flops 30720 | bytes 13312 | tf_op jit(solution)/shard_map/add | solution.py:20
  6.0 0.5 %collective-permute-done = s32[3,128]{1,0:T(4,128)S(1)} collective-permute-done((s32[3,128]{1,0:T(4,128)S(1)}, s32[3,128]{1,0:T(4,128)S(1)}, u32[]{:S(2)}, u32[]{:S(2)}) %collective-permute-start) | collective-permute-done | bytes 1568 | tf_op jit(solution)/shard_map/ppermute | solution.py:167
  6.5 0.1 dynamic-slice_add_fusion.1
  6.6 0.1 add.345.cp
  6.7 0.0 copy-start
  6.7 0.9 %copy-done = f32[10,2048]{1,0:T(8,128)S(1)} copy-done((f32[10,2048]{1,0:T(8,128)S(1)}, f32[10,2048]{1,0:T(8,128)}, u32[]{:S(2)}) %copy-start) | copy-done | bytes 81944
  7.6 0.0 copy-start.1
  7.6 0.7 %copy-done.1 = f32[2048]{0:T(1024)S(1)} copy-done((f32[2048]{0:T(1024)S(1)}, f32[2048]{0:T(1024)}, u32[]{:S(2)}) %copy-start.1) | copy-done | bytes 8216
  8.3 4.5 %basis_gram.1 = (f32[128,384]{1,0:T(8,128)S(1)}, f32[384,2048]{1,0:T(8,128)S(1)}) custom-call(s32[3,128]{1,0:T(4,128)S(1)} %add.345.cp, s32[3,256]{1,0:T(4,128)S(1)} %add_multiply_fusion.ct, f32[10,2048]{1,0:T(8,128)S(1)} %copy-done, f32[16,128]{1,0:T(8,128)S(1)} %bitcast.1), custom_call_target="tpu_custom_call" | custom-call | tf_op jit(solution)/shard_map/basis_gram/pallas_call | solution.py:211
  12.9 0.1 collective-permute-start.1
  13.0 1.3 %collective-permute-done.1 = f32[64,384]{1,0:T(8,128)S(1)} collective-permute-done((f32[64,384]{1,0:T(8,128)S(1)}, f32[64,384]{1,0:T(8,128)S(1)}, u32[]{:S(2)}, u32[]{:S(2)}) %collective-permute-start.1) | collective-permute-done | bytes 98336 | tf_op jit(solution)/shard_map/ppermute | solution.py:185
  14.3 2.0 %collective-permute-start.2 = (f32[64,384]{1,0:T(8,128)S(1)}, f32[64,384]{1,0:T(8,128)S(1)}, u32[]{:S(2)}, u32[]{:S(2)}) collective-permute-start(f32[64,384]{1,0:T(8,128)S(1)} %dynamic-slice_add_fusion), channel_id=1, source_target_pairs={{0,4},{2,6},{4,0},{6,2},{8,12},{10,14},{12,8},{14,10},{16,20},{18,... | collective-permute-start | bytes 294920 | tf_op jit(solution)/shard_map/ppermute | solution.py:167
  16.2 3.1 %collective-permute-done.2 = f32[64,384]{1,0:T(8,128)S(1)} collective-permute-done((f32[64,384]{1,0:T(8,128)S(1)}, f32[64,384]{1,0:T(8,128)S(1)}, u32[]{:S(2)}, u32[]{:S(2)}) %collective-permute-start.2) | collective-permute-done | bytes 98336 | tf_op jit(solution)/shard_map/ppermute | solution.py:167
  19.4 1.9 %collective-permute-start.3 = (f32[64,384]{1,0:T(8,128)S(1)}, f32[64,384]{1,0:T(8,128)S(1)}, u32[]{:S(2)}, u32[]{:S(2)}) collective-permute-start(f32[64,384]{1,0:T(8,128)S(1)} %add.381), channel_id=1, source_target_pairs={{0,8},{2,10},{4,12},{6,14},{8,0},{10,2},{12,4},{14,6},{16,24},{18,... | collective-permute-start | bytes 294920 | tf_op jit(solution)/shard_map/ppermute | solution.py:167
  21.3 2.8 %collective-permute-done.3 = f32[64,384]{1,0:T(8,128)S(1)} collective-permute-done((f32[64,384]{1,0:T(8,128)S(1)}, f32[64,384]{1,0:T(8,128)S(1)}, u32[]{:S(2)}, u32[]{:S(2)}) %collective-permute-start.3) | collective-permute-done | bytes 98336 | tf_op jit(solution)/shard_map/ppermute | solution.py:167
  24.1 2.9 %collective-permute-start.4 = (f32[64,384]{1,0:T(8,128)S(1)}, f32[64,384]{1,0:T(8,128)S(1)}, u32[]{:S(2)}, u32[]{:S(2)}) collective-permute-start(f32[64,384]{1,0:T(8,128)S(1)} %add.382), channel_id=1, source_target_pairs={{0,16},{2,18},{4,20},{6,22},{8,24},{10,26},{12,28},{14,30},{16,0},... | collective-permute-start | bytes 294920 | tf_op jit(solution)/shard_map/ppermute | solution.py:167
  27.0 2.7 %collective-permute-done.4 = f32[64,384]{1,0:T(8,128)S(1)} collective-permute-done((f32[64,384]{1,0:T(8,128)S(1)}, f32[64,384]{1,0:T(8,128)S(1)}, u32[]{:S(2)}, u32[]{:S(2)}) %collective-permute-start.4) | collective-permute-done | bytes 98336 | tf_op jit(solution)/shard_map/ppermute | solution.py:167
  29.7 0.1 collective-permute-start.5
  29.8 1.3 %collective-permute-done.5 = f32[64,384]{1,0:T(8,128)S(1)} collective-permute-done((f32[64,384]{1,0:T(8,128)S(1)}, f32[64,384]{1,0:T(8,128)S(1)}, u32[]{:S(2)}, u32[]{:S(2)}) %collective-permute-start.5) | collective-permute-done | bytes 98336 | tf_op jit(solution)/shard_map/ppermute | solution.py:187
  31.1 9.5 %factor.1 = (f32[128,128]{1,0:T(8,128)}, f32[128,256]{1,0:T(8,128)}, f32[128,256]{1,0:T(8,128)S(1)}) custom-call(f32[128,384]{1,0:T(8,128)S(1)} %maximum_select_fusion.total_ref), custom_call_target="tpu_custom_call" | custom-call | tf_op jit(solution)/shard_map/factor/pallas_call | solution.py:227
  40.6 4.5 %update.1 = f32[2048,256]{1,0:T(8,128)} custom-call(f32[384,2048]{1,0:T(8,128)S(1)} %get-tuple-element.11.basis, f32[128,256]{1,0:T(8,128)S(1)} %get-tuple-element.12.mix), custom_call_target="tpu_custom_call" | custom-call | tf_op jit(solution)/shard_map/update/pallas_call | solution.py:241
  (9 shorter events, 0.1 us)
Async XLA Ops:
  1.8 4.7 %collective-permute-start = (s32[3,128]{1,0:T(4,128)S(1)}, s32[3,128]{1,0:T(4,128)S(1)}, u32[]{:S(2)}, u32[]{:S(2)}) collective-permute-start(s32[3,128]{1,0:T(4,128)S(1)} %dynamic_update_slice.5), channel_id=1, source_target_pairs={{0,1},{1,0},{2,3},{3,2},{4,5},{5,4},{6,7},{7,6},{8,9},{9,8},{10,11... | collective-permute-start | bytes 4616 | tf_op jit(solution)/shard_map/ppermute | solution.py:167
  6.7 0.9 %copy-start = (f32[10,2048]{1,0:T(8,128)S(1)}, f32[10,2048]{1,0:T(8,128)}, u32[]{:S(2)}) copy-start(f32[10,2048]{1,0:T(8,128)} %pts.1) | copy-start | bytes 245764
  7.6 0.7 %copy-start.1 = (f32[2048]{0:T(1024)S(1)}, f32[2048]{0:T(1024)}, u32[]{:S(2)}) copy-start(f32[2048]{0:T(1024)} %param.5) | copy-start | bytes 24580
  12.9 1.4 %collective-permute-start.1 = (f32[64,384]{1,0:T(8,128)S(1)}, f32[64,384]{1,0:T(8,128)S(1)}, u32[]{:S(2)}, u32[]{:S(2)}) collective-permute-start(f32[64,384]{1,0:T(8,128)S(1)} %constant_dynamic-slice_fusion), channel_id=1, source_target_pairs={{0,2},{2,0},{4,6},{6,4},{8,10},{10,8},{12,14},{14,12},{16,18},{18,... | collective-permute-start | bytes 294920 | tf_op jit(solution)/shard_map/ppermute | solution.py:185
  14.3 5.1 %collective-permute-start.2 = (f32[64,384]{1,0:T(8,128)S(1)}, f32[64,384]{1,0:T(8,128)S(1)}, u32[]{:S(2)}, u32[]{:S(2)}) collective-permute-start(f32[64,384]{1,0:T(8,128)S(1)} %dynamic-slice_add_fusion), channel_id=1, source_target_pairs={{0,4},{2,6},{4,0},{6,2},{8,12},{10,14},{12,8},{14,10},{16,20},{18,... | collective-permute-start | bytes 294920 | tf_op jit(solution)/shard_map/ppermute | solution.py:167
  19.4 4.7 %collective-permute-start.3 = (f32[64,384]{1,0:T(8,128)S(1)}, f32[64,384]{1,0:T(8,128)S(1)}, u32[]{:S(2)}, u32[]{:S(2)}) collective-permute-start(f32[64,384]{1,0:T(8,128)S(1)} %add.381), channel_id=1, source_target_pairs={{0,8},{2,10},{4,12},{6,14},{8,0},{10,2},{12,4},{14,6},{16,24},{18,... | collective-permute-start | bytes 294920 | tf_op jit(solution)/shard_map/ppermute | solution.py:167
  24.1 5.6 %collective-permute-start.4 = (f32[64,384]{1,0:T(8,128)S(1)}, f32[64,384]{1,0:T(8,128)S(1)}, u32[]{:S(2)}, u32[]{:S(2)}) collective-permute-start(f32[64,384]{1,0:T(8,128)S(1)} %add.382), channel_id=1, source_target_pairs={{0,16},{2,18},{4,20},{6,22},{8,24},{10,26},{12,28},{14,30},{16,0},... | collective-permute-start | bytes 294920 | tf_op jit(solution)/shard_map/ppermute | solution.py:167
  29.7 1.4 %collective-permute-start.5 = (f32[64,384]{1,0:T(8,128)S(1)}, f32[64,384]{1,0:T(8,128)S(1)}, u32[]{:S(2)}, u32[]{:S(2)}) collective-permute-start(f32[64,384]{1,0:T(8,128)S(1)} %add.383), channel_id=1, source_target_pairs={{0,2},{2,0},{4,6},{6,4},{8,10},{10,8},{12,14},{14,12},{16,18},{18,... | collective-permute-start | bytes 294920 | tf_op jit(solution)/shard_map/ppermute | solution.py:187

commit v2 on v0

v2 whole, which is shorter than its diff:
```python
import functools
import math

import jax
import jax.numpy as jnp
from jax import lax
from jax.experimental import pallas as pl
from jax.experimental.pallas import tpu as pltpu
from jax.sharding import PartitionSpec as P

DEG = 6
LANES = 128
BLOCK = 8
F32 = jnp.float32
BF16 = jnp.bfloat16
VMEM_LIMIT = 16 << 20


def rank3(a, b, c):
    all3, last2 = a + b + c, b + c
    return (all3 * (all3 + 1) * (all3 + 2) * 10923 >> 16) + (last2 * (last2 + 1) >> 1) + c


def rank4(a, b, c, d):
    all4 = a + b + c + d
    return (all4 * (all4 + 1) * (all4 + 2) * (all4 + 3) * 2731 >> 16) + rank3(b, c, d)


COUNT3 = rank3(0, 0, DEG) + 1
COUNT4 = rank4(0, 0, 0, DEG) + 1


def codes(degrees, rows):
    d = [degrees[i : i + 1, :] for i in range(degrees.shape[0])]
    return [rows * rank3(*d[0:3]), rows * rank3(*d[3:6]), rows * rank4(*d[6:10])]


def split2(x):
    high = x.astype(BF16)
    return high, (x - high.astype(F32)).astype(BF16)


def product(left, right, dims):
    return lax.dot_general(left, right, (dims, ((), ())), preferred_element_type=F32)


def dot3(left, right, dims):
    (lh, ll), (rh, rl) = split2(left), split2(right)
    return product(lh, rh, dims) + product(lh, rl, dims) + product(ll, rh, dims)


def levels(p):
    one = jnp.ones_like(p)
    v = [one, p]
    for k in range(1, DEG):
        v.append(((2.0 * k + 1.0) * p * v[k] - float(k) * v[k - 1]) * (1.0 / (k + 1.0)))
    return [one] + [v[k] * math.sqrt(2.0 * k + 1.0) for k in range(1, DEG + 1)]


def times(x, factor, degree):
    return x * factor[degree] if degree else x


def select(tabs, code, count, out, rows):
    for j in range(count):
        starts = [pl.multiple_of(c(j), rows) for c in code]
        a, b, c = (tab[pl.ds(s, rows), :] for tab, s in zip(tabs, starts))
        out[j * rows : (j + 1) * rows, :] = a * b * c


def tables(run_total, own_hbm, deg_hbm, pts_hbm, wts_hbm, tab_a, tab_b, tab_c, sel, own, deg, pts, wts, coord, code, code_smem, sem):
    pairs = ((deg_hbm, deg), (pts_hbm, pts), (wts_hbm, wts), (own_hbm, own))
    copies = [pltpu.make_async_copy(src, dst, sem.at[i]) for i, (src, dst) in enumerate(pairs)]
    for copy in copies:
        copy.start()
    count, rows = deg.shape[1], wts.shape[0]
    copies[0].wait()
    for g, value in enumerate(codes(deg[...], rows)):
        code[g : g + 1, :] = value
    to_scalars = pltpu.make_async_copy(code, code_smem, sem.at[len(pairs)])
    to_scalars.start()
    for copy in copies[1:]:
        copy.wait()
    for d in range(pts.shape[0]):
        for i in range(rows):
            coord[pl.ds(d * rows + i, 1), :] = pts[pl.ds(d, 1), pl.ds(i * LANES, LANES)]
    scale = jnp.sqrt(wts[...] / run_total)
    lv = [levels(coord[pl.ds(d * rows, rows), :]) for d in range(pts.shape[0])]

    def put(table, rank, value):
        table[pl.ds(rank * rows, rows), :] = value

    for table, d, first in ((tab_a, 0, scale), (tab_b, 3, jnp.ones_like(scale))):
        for a in range(DEG + 1):
            xa = times(first, lv[d], a)
            for b in range(DEG + 1 - a):
                xb = times(xa, lv[d + 1], b)
                for c in range(DEG + 1 - a - b):
                    put(table, rank3(a, b, c), times(xb, lv[d + 2], c))
    for a in range(DEG + 1):
        xa = lv[6][a]
        for b in range(DEG + 1 - a):
            xb = times(xa, lv[7], b)
            for c in range(DEG + 1 - a - b):
                xc = times(xb, lv[8], c)
                for d in range(DEG + 1 - a - b - c):
                    put(tab_c, rank4(a, b, c, d), times(xc, lv[9], d))
    to_scalars.wait()
    select((tab_a, tab_b, tab_c), [lambda j, g=g: code_smem[g, j] for g in range(3)], count, sel, rows)


def inner(rows, ca, cb, cc, tab_a, tab_b, tab_c, trail, gram, panel):
    width, others = ca.shape[0], trail.shape[0] // rows
    select((tab_a, tab_b, tab_c), [lambda j, c=c: c[j] for c in (ca, cb, cc)], width, panel, rows)
    acc = jnp.zeros((width, width + others), F32)
    for i in range(rows // 2):
        p, t = (
            jnp.concatenate([ref[pl.ds(2 * i + h, n, stride=rows), :] for h in range(2)], axis=1)
            for ref, n in ((panel, width), (trail, others))
        )
        ph, plo = split2(p)
        th, tlo = split2(t)
        high = jnp.concatenate([ph, th], axis=0)
        low = jnp.concatenate([plo, tlo], axis=0)
        dims = ((1,), (1,))
        acc = acc + product(ph, high, dims) + product(ph, low, dims) + product(plo, high, dims)
    gram[...] = acc


def by_sample(rows, scale, panel, trail, panel_halves, trail_rows):
    width, others = panel.shape[0] // rows, trail.shape[0] // rows
    for i in range(rows):
        here = pl.ds(i * LANES, LANES)
        high, low = split2(panel[pl.ds(i, width, stride=rows), :].T)
        panel_halves[here, :width] = high
        panel_halves[here, width:] = low
        trail_rows[here, :] = trail[pl.ds(i, others, stride=rows), :].T * scale


def tree(terms):
    while len(terms) > 1:
        odd = terms[-1:] if len(terms) % 2 else []
        terms = [a + b for a, b in zip(terms[::2], terms[1::2])] + odd
    return terms[0]


def small_factor(col):
    size, shape = len(col), col[0].shape
    e = {(r, c): jnp.broadcast_to(col[c][r : r + 1, :], shape) for c in range(size) for r in range(c, size)}
    x, z = {}, {}
    for r in range(size):
        inv = lax.rsqrt(e[r, r])
        for c in range(r):
            x[r, c] = z[r, c] * inv
        x[r, r] = inv
        l = {q: e[q, r] * inv for q in range(r + 1, size)}
        for q in range(r + 1, size):
            for c in range(r + 1, q + 1):
                e[q, c] = e[q, c] - l[q] * l[c]
            for c in range(r + 1):
                term = l[q] * x[r, c]
                z[q, c] = z[q, c] - term if (q, c) in z else -term
    return x


def factor_rows(a):
    b, blocks, n = BLOCK, len(a), a[0].shape[1]
    sub = lax.broadcasted_iota(jnp.int32, (b, n), 0)
    lane = lax.broadcasted_iota(jnp.int32, (b, n), 1)

    def over_lanes(v, j):
        return jnp.broadcast_to(v[:, j : j + 1], (b, n))

    def over_rows(v, r):
        return jnp.broadcast_to(v[r : r + 1, :], (b, n))

    zero = jnp.zeros((b, n), F32)
    upper, inverse = [], []
    col = [over_lanes(a[0], c) + 0.0 for c in range(b)]
    for k in range(blocks):
        lo, last = k * b, k + 1 == blocks
        f = {i: [over_lanes(a[i], lo + m) for m in range(b)] for i in range(k + 1, blocks)}
        x_col = None if last else [over_lanes(a[k + 1], lo + b + c) for c in range(b)]
        x = small_factor(col)
        if not last:
            v = [tree([f[k + 1][m] * x[c, m] for m in range(c + 1)]) for c in range(b)]
            col = [x_col[c] - tree([v[m] * over_rows(v[m], c) for m in range(b)]) for c in range(b)]
        down, across = [], []
        for c in range(b):
            p, q = zero, zero
            for r in range(c, b):
                p = jnp.where(sub == r, x[r, c], p)
            for m in range(c + 1):
                q = jnp.where(sub == m, x[c, m], q)
            down.append(p)
            across.append(q)
        t = tree([down[c] * over_rows(a[k], c) for c in range(b)])
        upper.append(jnp.where(lane >= lo + sub, t, 0.0))
        full = t
        for c in range(b):
            full = jnp.where(lane == lo + c, down[c], full)
        inverse.append(jnp.where(lane < lo + b, full, 0.0))
        if not last:
            y = tree([across[c] * over_rows(full, c) for c in range(b)])
            y_rows = [over_rows(y, m) for m in range(b)]
            inside = (lane >= lo) & (lane < lo + b)
            for i in range(k + 1, blocks):
                a[i] = jnp.where(inside, 0.0, a[i]) - tree([f[i][m] * y_rows[m] for m in range(b)])
    return upper, inverse


def finish(scale, total, panel_halves, trail_rows, r_out, coupling_out, updated_out, r_buf, c_buf, w_buf, u_buf, sem):
    n = total.shape[0]
    upper, inverse = factor_rows([total[i : i + BLOCK, :n] for i in range(0, n, BLOCK)])
    for i in range(n // BLOCK):
        r_buf[i * BLOCK : (i + 1) * BLOCK, :] = upper[i]
        w_buf[i * BLOCK : (i + 1) * BLOCK, :] = inverse[i]
    copies = [pltpu.make_async_copy(r_buf, r_out, sem.at[0])]
    copies[0].start()
    w = w_buf[...]
    coupling = dot3(w, total[:, n:], ((1,), (0,)))
    c_buf[...] = coupling
    copies.append(pltpu.make_async_copy(c_buf, coupling_out, sem.at[1]))
    copies[1].start()
    high, low = split2(scale * dot3(w, coupling, ((0,), (0,))))
    twice = jnp.concatenate([high, high], axis=0)
    runs = u_buf.shape[0]
    tile = 2 * LANES
    for i in range(runs // tile):
        here = pl.ds(i * tile, tile)
        dims = ((1,), (0,))
        u_buf[here, :] = trail_rows[here, :] - (
            product(panel_halves[here, :], twice, dims) + product(panel_halves[here, :n], low, dims)
        )
        copies.append(pltpu.make_async_copy(u_buf.at[here], updated_out.at[here], sem.at[2 + i]))
        copies[-1].start()
    for copy in copies:
        copy.wait()


def powers(size):
    return [1 << b for b in range(size.bit_length() - 1)]


def swapped(x, axis, step):
    return lax.ppermute(x, axis, [(i, i ^ step) for i in range(lax.axis_size(axis))])


def in_order(mine, other, first, dim):
    return jnp.where(first, jnp.concatenate([mine, other], dim), jnp.concatenate([other, mine], dim))


def all_sum(x, axis):
    size = lax.axis_size(axis)
    if size & (size - 1):
        return lax.psum(x, axis)
    if size == 1:
        return x
    half = x.shape[0] // 2
    odd = lax.axis_index(axis) % 2
    mine = lax.dynamic_slice_in_dim(x, odd * half, half, 0)
    mine = mine + swapped(lax.dynamic_slice_in_dim(x, (1 - odd) * half, half, 0), axis, 1)
    for step in powers(size)[1:]:
        mine = mine + swapped(mine, axis, step)
    return in_order(mine, swapped(mine, axis, 1), odd == 0, 0)


def gather_columns(x, near, axis):
    size = lax.axis_size(axis)
    if size & (size - 1):
        return lax.all_gather(x, axis, axis=1, tiled=True)
    for step in powers(size):
        other = swapped(x, axis, step)
        x = in_order(near if step == 1 else x, other, lax.axis_index(axis) & step == 0, 1)
    return x


def call(kernel, name, outs, in_specs, out_specs, scratch, args, flops, moved):
    return pl.pallas_call(
        kernel,
        out_shape=[jax.ShapeDtypeStruct(*o) for o in outs],
        in_specs=in_specs,
        out_specs=out_specs,
        scratch_shapes=scratch,
        compiler_params=pltpu.CompilerParams(vmem_limit_bytes=VMEM_LIMIT),
        cost_estimate=pl.CostEstimate(flops=flops, bytes_accessed=moved, transcendentals=0),
        name=name,
    )(*args)


def shards(points, run_weights, panel_degrees, trailing_degrees):
    dims, runs = points.shape
    rows = runs // LANES
    run_total = runs * lax.axis_size("sample")
    scale = math.sqrt(run_total)
    smem = pl.BlockSpec(memory_space=pltpu.SMEM)
    vmem = pl.BlockSpec(memory_space=pltpu.VMEM)
    far = pl.BlockSpec(memory_space=pltpu.HBM)
    own_width, others = panel_degrees.shape[1], trailing_degrees.shape[1]
    width = own_width * lax.axis_size("basis")
    total = width + others
    *tabs, trail, own_degrees = call(
        functools.partial(tables, float(run_total)),
        "tables",
        [((c * rows, LANES), F32) for c in (COUNT3, COUNT3, COUNT4, others)] + [((dims, own_width), jnp.int32)],
        [far] * 4,
        [vmem] * 5,
        [
            pltpu.VMEM((dims, others), jnp.int32),
            pltpu.VMEM((dims, runs), F32),
            pltpu.VMEM((rows, LANES), F32),
            pltpu.VMEM((dims * rows, LANES), F32),
            pltpu.VMEM((BLOCK, others), jnp.int32),
            pltpu.SMEM((BLOCK, others), jnp.int32),
            pltpu.SemaphoreType.DMA((5,)),
        ],
        [
            pltpu.with_memory_space_constraint(x, pltpu.HBM)
            for x in (panel_degrees, trailing_degrees, points, run_weights.reshape(rows, LANES))
        ],
        runs * 1000,
        runs * 2000,
    )
    all_degrees = gather_columns(panel_degrees, own_degrees, "basis")
    gram, panel = call(
        functools.partial(inner, rows),
        "inner",
        [((width, total), F32), ((width * rows, LANES), F32)],
        [smem] * 3 + [vmem] * 4,
        [vmem] * 2,
        [],
        (*(c[0] for c in codes(all_degrees, rows)), *tabs, trail),
        6 * width * total * runs,
        4 * runs * total,
    )
    panel_halves, trail_rows = call(
        functools.partial(by_sample, rows, scale),
        "by_sample",
        [((runs, 2 * width), BF16), ((runs, others), F32)],
        [vmem] * 2,
        [vmem] * 2,
        [],
        (panel, trail),
        runs * total,
        8 * runs * total,
    )
    sums = all_sum(gram, "sample")
    r_factor, coupling, updated = call(
        functools.partial(finish, scale),
        "finish",
        [((width, width), F32), ((width, others), F32), ((runs, others), F32)],
        [vmem] * 3,
        [far] * 3,
        [
            pltpu.VMEM((width, width), F32),
            pltpu.VMEM((width, others), F32),
            pltpu.VMEM((width, width), F32),
            pltpu.VMEM((runs, others), F32),
            pltpu.SemaphoreType.DMA((2 + runs // (2 * LANES),)),
        ],
        (sums, panel_halves, trail_rows),
        6 * width * others * runs,
        8 * runs * total,
    )
    return (r_factor, coupling, updated)


def solution(mesh):
    in_specs = (P(None, "sample"), P("sample"), P(None, "basis"), P(None, "basis"))
    out_specs = (P(), P(None, "basis"), P("sample", "basis"))
    return jax.shard_map(shards, mesh=mesh, in_specs=in_specs, out_specs=out_specs, check_vma=False)
```

time: 178 us -> 32.6 us (0.18)
  waiting for transfers between devices: 104 us -> 9.87 us
  other arithmetic: 28.3 us -> 0.16 us
  matrix products: 26.5 us -> 0 us
  between operations: 14.4 us -> 0.74 us
  Pallas kernels: 0 us -> 11.2 us
  starting transfers between devices: 0.26 us -> 10 us
  local copies, waits for them, and re-layouts: 3.65 us -> 0.02 us
    psum x1 -> x0, waiting for transfers between devices: 91 us -> none  [shards(): lax.psum((inner_products(panel, panel), inner_products(panel, trailing)),...]
    dot_general x25 -> x0, matrix products: 26.2 us -> none  [the longest x20 15.6 us: weighted_columns(): lax.dot_general(table, selector, (((0,), (0,)), ((), ())), precision=lax....]
    another operation x5 -> x0, other arithmetic: 22.9 us -> none  [the longest x3 12.4 us: shards(): lower_factor = jnp.linalg.cholesky(gram_matrix)]
    all_gather x1 -> x0, waiting for transfers between devices: 13.2 us -> none  [shards(): panel = lax.all_gather(own_columns, 'basis', axis=1, tiled=True)]
    pallas_call x0 -> x4, Pallas kernels: none -> 11.2 us  [call(): pl.pallas_call(kernel, out_shape=[jax.ShapeDtypeStruct(*o) for o in outs]...]
    ppermute x0 -> x6, starting transfers between devices: none -> 10 us  [swapped(): lax.ppermute(x, axis, [(i, i ^ step) for i in range(lax.axis_size(axis))])]
    ppermute x0 -> x6, waiting for transfers between devices: none -> 9.87 us  [swapped(): lax.ppermute(x, axis, [(i, i ^ step) for i in range(lax.axis_size(axis))])]
    mul x17 -> x0, other arithmetic: 3.87 us -> none  [legendre_rows(): values[degree] * math.sqrt(2.0 * degree + 1.0)]
  transfers between devices with their start and end apart: 2 -> 6, of which waited for: 2 -> 4; matrix products, arithmetic and copies ran while one was open for 6% -> 0% of each run, Pallas kernels for 0% -> 10%
where the time goes in v2:
time: 32.6 us; the launch traced here: 32 us
  Pallas kernels  11.2 us (34%)
  starting transfers between devices  10 us (31%)
  waiting for transfers between devices  9.87 us (30%)
  between operations  0.74 us (2%)
    pallas_call x4, Pallas kernels, call(): pl.pallas_call(kernel, out_shape=[jax.ShapeDtypeStruct(*o) for o in outs]...  11.2 us
    ppermute x6, starting transfers between devices, swapped(): lax.ppermute(x, axis, [(i, i ^ step) for i in range(lax.axis_size(axis))])  10 us
    ppermute x6, waiting for transfers between devices, swapped(): lax.ppermute(x, axis, [(i, i ^ step) for i in range(lax.axis_size(axis))])  9.87 us
  transfers between devices with their start and end apart: 6, of which 4 were waited for; matrix products, arithmetic and copies ran while one was open for 0% of the time, Pallas kernels for 10%

profile of v2, /device:TPU:0, one launch (start us, length us, event | category | flops | bytes accessed | tf_op | source)
XLA Modules:
  0.0 32.0 jit_solution(16931507970009789748)
XLA Ops:
  0.6 3.1 %collective-permute-start = (s32[10,64]{1,0:T(8,128)}, s32[10,64]{1,0:T(8,128)S(1)}, u32[]{:S(2)}, u32[]{:S(2)}) collective-permute-start(s32[10,64]{1,0:T(8,128)} %own_hbm.1), channel_id=1, source_target_pairs={{0,1},{1,0},{2,3},{3,2},{4,5},{5,4},{6,7},{7,6},{8,9},{9,8},{10,11... | collective-permute-start | bytes 7688 | tf_op jit(solution)/shard_map/ppermute | solution.py:246
  3.7 1.9 %tables.1 = (f32[1344,128]{1,0:T(8,128)S(1)}, f32[1344,128]{1,0:T(8,128)S(1)}, f32[3360,128]{1,0:T(8,128)S(1)}, f32[4096,128]{1,0:T(8,128)S(1)}, s32[10,64]{1,0:T(8,128)S(1)}) custom-call(s32[10,64]{1,0:T(8,128)} %own_hbm.1, s32[10,256]{1,0:T(8,128)} %deg_hbm.1, f32[10,2048]{1,0:T(8,128)} %pts_hbm.1, f32[16,128]{1,0:T(8,128)} %bitcast.7), custom_call_target="tpu_custom_call" | custom-call | flops 2048000 | bytes 4096000 | tf_op jit(solution)/shard_map/tables/pallas_call | solution.py:279
  5.6 0.0 collective-permute-done
  5.6 0.1 add_select_fusion
  5.7 2.7 %inner.1 = (f32[128,384]{1,0:T(8,128)S(1)}, f32[2048,128]{1,0:T(8,128)S(1)}) custom-call(s32[128]{0:T(128)S(1)} %get-tuple-element.23.ca, s32[128]{0:T(128)S(1)} %get-tuple-element.22.cb, s32[128]{0:T(128)S(1)} %get-tuple-element.21.cc, f32[1344,128]{1,0:T(8,128)S(1)} %get-tuple-element.13.tab_a, f32[1344,128]{1,0:T(8,128)S(1)} %get-tuple-element.14.tab_b, ...), custom_call_target="tpu_custom_call" | custom-call | flops 603979776 | bytes 3145728 | tf_op jit(solution)/shard_map/inner/pallas_call | solution.py:279
  8.4 0.1 collective-permute-start.1
  8.5 1.3 %collective-permute-done.1 = f32[64,384]{1,0:T(8,128)S(1)} collective-permute-done((f32[64,384]{1,0:T(8,128)S(1)}, f32[64,384]{1,0:T(8,128)S(1)}, u32[]{:S(2)}, u32[]{:S(2)}) %collective-permute-start.1) | collective-permute-done | bytes 98336 | tf_op jit(solution)/shard_map/ppermute | solution.py:246
  9.8 2.0 %collective-permute-start.2 = (f32[64,384]{1,0:T(8,128)S(1)}, f32[64,384]{1,0:T(8,128)S(1)}, u32[]{:S(2)}, u32[]{:S(2)}) collective-permute-start(f32[64,384]{1,0:T(8,128)S(1)} %dynamic-slice_add_fusion), channel_id=1, source_target_pairs={{0,4},{2,6},{4,0},{6,2},{8,12},{10,14},{12,8},{14,10},{16,20},{18,... | collective-permute-start | bytes 294920 | tf_op jit(solution)/shard_map/ppermute | solution.py:246
  11.8 3.1 %collective-permute-done.2 = f32[64,384]{1,0:T(8,128)S(1)} collective-permute-done((f32[64,384]{1,0:T(8,128)S(1)}, f32[64,384]{1,0:T(8,128)S(1)}, u32[]{:S(2)}, u32[]{:S(2)}) %collective-permute-start.2) | collective-permute-done | bytes 98336 | tf_op jit(solution)/shard_map/ppermute | solution.py:246
  14.9 1.9 %collective-permute-start.3 = (f32[64,384]{1,0:T(8,128)S(1)}, f32[64,384]{1,0:T(8,128)S(1)}, u32[]{:S(2)}, u32[]{:S(2)}) collective-permute-start(f32[64,384]{1,0:T(8,128)S(1)} %add.154), channel_id=1, source_target_pairs={{0,8},{2,10},{4,12},{6,14},{8,0},{10,2},{12,4},{14,6},{16,24},{18,... | collective-permute-start | bytes 294920 | tf_op jit(solution)/shard_map/ppermute | solution.py:246
  16.8 2.8 %collective-permute-done.3 = f32[64,384]{1,0:T(8,128)S(1)} collective-permute-done((f32[64,384]{1,0:T(8,128)S(1)}, f32[64,384]{1,0:T(8,128)S(1)}, u32[]{:S(2)}, u32[]{:S(2)}) %collective-permute-start.3) | collective-permute-done | bytes 98336 | tf_op jit(solution)/shard_map/ppermute | solution.py:246
  19.6 2.9 %collective-permute-start.4 = (f32[64,384]{1,0:T(8,128)S(1)}, f32[64,384]{1,0:T(8,128)S(1)}, u32[]{:S(2)}, u32[]{:S(2)}) collective-permute-start(f32[64,384]{1,0:T(8,128)S(1)} %add.155), channel_id=1, source_target_pairs={{0,16},{2,18},{4,20},{6,22},{8,24},{10,26},{12,28},{14,30},{16,0},... | collective-permute-start | bytes 294920 | tf_op jit(solution)/shard_map/ppermute | solution.py:246
  22.5 2.7 %collective-permute-done.4 = f32[64,384]{1,0:T(8,128)S(1)} collective-permute-done((f32[64,384]{1,0:T(8,128)S(1)}, f32[64,384]{1,0:T(8,128)S(1)}, u32[]{:S(2)}, u32[]{:S(2)}) %collective-permute-start.4) | collective-permute-done | bytes 98336 | tf_op jit(solution)/shard_map/ppermute | solution.py:246
  25.2 0.1 collective-permute-start.5
  25.3 1.3 %by_sample.1 = (bf16[2048,256]{1,0:T(8,128)(2,1)S(1)}, f32[2048,256]{1,0:T(8,128)S(1)}) custom-call(f32[2048,128]{1,0:T(8,128)S(1)} %get-tuple-element.18.panel, f32[4096,128]{1,0:T(8,128)S(1)} %get-tuple-element.16.trail), custom_call_target="tpu_custom_call" | custom-call | flops 786432 | bytes 6291456 | tf_op jit(solution)/shard_map/by_sample/pallas_call | solution.py:279
  26.7 0.0 collective-permute-done.5
  26.7 5.3 %finish.1 = (f32[128,128]{1,0:T(8,128)}, f32[128,256]{1,0:T(8,128)}, f32[2048,256]{1,0:T(8,128)}) custom-call(f32[128,384]{1,0:T(8,128)S(1)} %maximum_select_fusion.total, bf16[2048,256]{1,0:T(8,128)(2,1)S(1)} %get-tuple-element.19.panel_halves, f32[2048,256]{1,0:T(8,128)S(1)} %get-tuple-element.20.trail_rows), custom_call_target="tpu_custom_call" | custom-call | flops 402653184 | bytes 6291456 | tf_op jit(solution)/shard_map/finish/pallas_call | solution.py:279
  (7 shorter events, 0.1 us)
Async XLA Ops:
  0.6 4.9 %collective-permute-start = (s32[10,64]{1,0:T(8,128)}, s32[10,64]{1,0:T(8,128)S(1)}, u32[]{:S(2)}, u32[]{:S(2)}) collective-permute-start(s32[10,64]{1,0:T(8,128)} %own_hbm.1), channel_id=1, source_target_pairs={{0,1},{1,0},{2,3},{3,2},{4,5},{5,4},{6,7},{7,6},{8,9},{9,8},{10,11... | collective-permute-start | bytes 7688 | tf_op jit(solution)/shard_map/ppermute | solution.py:246
  8.4 1.4 %collective-permute-start.1 = (f32[64,384]{1,0:T(8,128)S(1)}, f32[64,384]{1,0:T(8,128)S(1)}, u32[]{:S(2)}, u32[]{:S(2)}) collective-permute-start(f32[64,384]{1,0:T(8,128)S(1)} %constant_dynamic-slice_fusion), channel_id=1, source_target_pairs={{0,2},{2,0},{4,6},{6,4},{8,10},{10,8},{12,14},{14,12},{16,18},{18,... | collective-permute-start | bytes 294920 | tf_op jit(solution)/shard_map/ppermute | solution.py:246
  9.8 5.1 %collective-permute-start.2 = (f32[64,384]{1,0:T(8,128)S(1)}, f32[64,384]{1,0:T(8,128)S(1)}, u32[]{:S(2)}, u32[]{:S(2)}) collective-permute-start(f32[64,384]{1,0:T(8,128)S(1)} %dynamic-slice_add_fusion), channel_id=1, source_target_pairs={{0,4},{2,6},{4,0},{6,2},{8,12},{10,14},{12,8},{14,10},{16,20},{18,... | collective-permute-start | bytes 294920 | tf_op jit(solution)/shard_map/ppermute | solution.py:246
  14.9 4.7 %collective-permute-start.3 = (f32[64,384]{1,0:T(8,128)S(1)}, f32[64,384]{1,0:T(8,128)S(1)}, u32[]{:S(2)}, u32[]{:S(2)}) collective-permute-start(f32[64,384]{1,0:T(8,128)S(1)} %add.154), channel_id=1, source_target_pairs={{0,8},{2,10},{4,12},{6,14},{8,0},{10,2},{12,4},{14,6},{16,24},{18,... | collective-permute-start | bytes 294920 | tf_op jit(solution)/shard_map/ppermute | solution.py:246
  19.6 5.6 %collective-permute-start.4 = (f32[64,384]{1,0:T(8,128)S(1)}, f32[64,384]{1,0:T(8,128)S(1)}, u32[]{:S(2)}, u32[]{:S(2)}) collective-permute-start(f32[64,384]{1,0:T(8,128)S(1)} %add.155), channel_id=1, source_target_pairs={{0,16},{2,18},{4,20},{6,22},{8,24},{10,26},{12,28},{14,30},{16,0},... | collective-permute-start | bytes 294920 | tf_op jit(solution)/shard_map/ppermute | solution.py:246
  25.2 1.4 %collective-permute-start.5 = (f32[64,384]{1,0:T(8,128)S(1)}, f32[64,384]{1,0:T(8,128)S(1)}, u32[]{:S(2)}, u32[]{:S(2)}) collective-permute-start(f32[64,384]{1,0:T(8,128)S(1)} %add.156), channel_id=1, source_target_pairs={{0,2},{2,0},{4,6},{6,4},{8,10},{10,8},{12,14},{14,12},{16,18},{18,... | collective-permute-start | bytes 294920 | tf_op jit(solution)/shard_map/ppermute | solution.py:246
